TPU v7x, 32 devices: a whole 2x2x4 slice. The times are simulated.
32 devices in a mesh: seq: 16 (over z, x, core), head: 2 (over y).
Axes of the slice: x: 2, y: 2, z: 4, core: 2. Of those that a mesh axis runs over, the one named last changes fastest.
Arguments:
- queries: bfloat16 [2, 1024, 4096], P(None, ('seq', 'head')), may hold values from -6 to 6
- keys: bfloat16 [2, 1024, 4096], P(None, ('seq', 'head')), may hold values from -6 to 6
- values: bfloat16 [2, 1024, 4096], P(None, ('seq', 'head')), may hold values from -6 to 6
- rates: bfloat16 [2, 1024, 8], P(None, ('seq', 'head')), may hold values from 0.049804688 to 1
- fast_init: float32 [8, 3, 512, 256], P('head', None, 'seq'), may hold values from -0.25 to 0.25
Outputs:
- outputs: bfloat16 [2, 1024, 4096], P(None, 'seq', 'head')
All inputs are finite; a program needn't handle non-finite values.
Results may differ from a plain program's by a relative error of at most 0.0085.
Values may be sent and summed in bfloat16 or wider, within the bound.
No kernel may reach another device: no remote copies, remote signals or barrier semaphores. Data moves between devices by JAX's collectives and lax.ppermute only.
A program may use at most 64 MiB of HBM per device.

v0:
```python
import jax
import jax.numpy as jnp
from jax import lax
from jax.sharding import PartitionSpec as P

EPSILON = 1e-06
COEF_A = 3.4445
COEF_B = -4.775
COEF_C = 2.0315
LEARNING_STEP = 0.5
FULL_PRECISION = lax.Precision.HIGHEST


def silu_parts(gate_pre):
    sigmoid_value = jax.nn.sigmoid(gate_pre)
    return (gate_pre * sigmoid_value, sigmoid_value * (1.0 + gate_pre * (1.0 - sigmoid_value)))


def local_gram(weight_matrices):
    return jnp.einsum("hmrf,hmrg->hmfg", weight_matrices, weight_matrices, precision=FULL_PRECISION)


def newton_schulz(gradients, gram_fn):
    gram_matrix = gram_fn(gradients)
    norm_value = jnp.sqrt(jnp.trace(gram_matrix, axis1=2, axis2=3)) + EPSILON
    current_weights = gradients / norm_value[:, :, None, None]
    gram_matrix = gram_matrix / (norm_value * norm_value)[:, :, None, None]
    identity = jnp.eye(gram_matrix.shape[-1], dtype=gram_matrix.dtype)
    for sweeps in range(2):
        if sweeps > 0:
            gram_matrix = gram_fn(current_weights)
        square = jnp.einsum("hmfg,hmgk->hmfk", gram_matrix, gram_matrix, precision=FULL_PRECISION)
        polynomial_update = COEF_A * identity + COEF_B * gram_matrix + COEF_C * square
        current_weights = jnp.einsum(
            "hmrf,hmfg->hmrg", current_weights, polynomial_update, precision=FULL_PRECISION
        )
    return current_weights


def local(queries, keys, values, rates, fast_init):
    weights = lax.all_gather(fast_init, "seq", axis=2, tiled=True)
    head_count = weights.shape[0]
    head_size = weights.shape[2]
    results = []
    for group_index in range(queries.shape[0]):
        query_flat, key_flat, value_flat, rate_rows = (
            lax.all_to_all(queries[group_index], "head", split_axis=1, concat_axis=0, tiled=True),
            lax.all_to_all(keys[group_index], "head", split_axis=1, concat_axis=0, tiled=True),
            lax.all_to_all(values[group_index], "head", split_axis=1, concat_axis=0, tiled=True),
            lax.all_to_all(rates[group_index], "head", split_axis=1, concat_axis=0, tiled=True),
        )
        row_count = query_flat.shape[0]
        query_rows = query_flat.reshape(row_count, head_count, head_size)
        key_rows = key_flat.reshape(row_count, head_count, head_size)
        value_rows = value_flat.reshape(row_count, head_count, head_size)
        low = weights.astype(jnp.bfloat16)
        gate_pre = jnp.einsum(
            "rhd,hdf->rhf", key_rows, low[:, 0], preferred_element_type=jnp.float32
        )
        up_proj = jnp.einsum(
            "rhd,hdf->rhf", key_rows, low[:, 1], preferred_element_type=jnp.float32
        )
        activated_hidden, slope_value = silu_parts(gate_pre)
        hidden = (activated_hidden * up_proj).astype(jnp.bfloat16)
        out_grad = (
            -(rate_rows.astype(jnp.float32)[:, :, None] * value_rows.astype(jnp.float32))
        ).astype(jnp.bfloat16)
        hidden_grad = jnp.einsum(
            "rhd,hdf->rhf", out_grad, low[:, 2], preferred_element_type=jnp.float32
        )
        gate_grad = (hidden_grad * up_proj * slope_value).astype(jnp.bfloat16)
        up_grad = (hidden_grad * activated_hidden).astype(jnp.bfloat16)
        gradients = jnp.stack(
            [
                jnp.einsum("rhd,rhf->hdf", key_rows, gate_grad, preferred_element_type=jnp.float32),
                jnp.einsum("rhd,rhf->hdf", key_rows, up_grad, preferred_element_type=jnp.float32),
                jnp.einsum("rhd,rhf->hdf", out_grad, hidden, preferred_element_type=jnp.float32),
            ],
            axis=1,
        )
        total_grad = lax.psum(gradients, "seq")
        update = newton_schulz(total_grad, local_gram)
        weights = weights - LEARNING_STEP * update
        low = weights.astype(jnp.bfloat16)
        query_gate = jnp.einsum(
            "rhd,hdf->rhf", query_rows, low[:, 0], preferred_element_type=jnp.float32
        )
        query_up = jnp.einsum(
            "rhd,hdf->rhf", query_rows, low[:, 1], preferred_element_type=jnp.float32
        )
        query_act, unused_slope = silu_parts(query_gate)
        query_hidden = (query_act * query_up).astype(jnp.bfloat16)
        result = jnp.einsum(
            "rhf,hdf->rhd", query_hidden, low[:, 2], preferred_element_type=jnp.float32
        )
        results.append(result.astype(jnp.bfloat16).reshape(row_count, head_count * head_size))
    return jnp.stack(results)


def solution(mesh):
    return jax.shard_map(
        local,
        mesh=mesh,
        in_specs=(
            P(None, ("seq", "head"), None),
            P(None, ("seq", "head"), None),
            P(None, ("seq", "head"), None),
            P(None, ("seq", "head"), None),
            P("head", None, "seq", None),
        ),
        out_specs=P(None, "seq", "head"),
        check_vma=False,
    )
```

profile of v0, /device:TPU:0, one launch (start us, length us, event | category | flops | bytes accessed | tf_op | source)
XLA Modules:
  0.0 496.7 jit_solution(14485534307048518920)
XLA Ops:
  6.5 1.8 copy.62
  8.4 1.3 fusion.99
  9.7 4.3 all-to-all-start
  16.0 1.7 all-to-all-done
  17.7 3.5 all-to-all-start.2
  22.2 4.1 all-to-all-done.2
  26.4 3.4 all-to-all-start.1
  30.1 4.8 all-to-all-done.1
  35.5 38.2 %all-gather.2.cloned.1.call-done = f32[4,3,512,256]{3,2,0,1:T(8,128)} async-done(((f32[4,3,32,256]{3,2,0,1:T(8,128)}), f32[4,3,512,256]{3,2,0,1:T(8,128)}) %all-gather.2.cloned.1.call-update) | async-done | bytes 6291472 | tf_op jit(solution)/shard_map/all_gather | solution.py:41
  73.7 3.1 convert_element_type.105
  79.3 3.3 pad_maximum_fusion
  82.6 3.2 all-to-all-start.4
  87.8 1.6 all-to-all-done.4
  89.5 3.4 all-to-all-start.5
  93.0 5.1 %all-to-all-done.5 = bf16[32,2,2048]{2,0,1:T(8,128)(2,1)S(1)} async-done(((bf16[32,2,2048]{2,0,1:T(8,128)(2,1)}), bf16[32,2,2048]{2,0,1:T(8,128)(2,1)S(1)}, u32[]{:S(2)}, u32[]{:S(2)}) %all-to-all-start.5) | async-done | bytes 262176 | tf_op jit(solution)/shard_map/all_to_all | solution.py:49
  98.1 3.4 all-to-all-start.6
  102.2 4.5 all-to-all-done.6
  108.5 112.3 %all-reduce.3.cloned.1.call-done = f32[4,3,512,256]{2,3,0,1:T(8,128)} async-done(((f32[4,3,512,256]{2,3,0,1:T(8,128)}), f32[4,3,512,256]{2,3,0,1:T(8,128)}) %all-reduce.3.cloned.1.call-update) | async-done | bytes 6291472 | tf_op jit(solution)/shard_map/psum | solution.py:81
  220.8 19.0 %select_reduce_fusion.1 = (f32[4,3]{1,0:T(4,128)S(1)}, f32[4,3,256,256]{3,2,1,0:T(8,128)}) fusion(pred[256,256]{1,0:T(8,128)(4,1)S(1)} %iota_compare_fusion, f32[4,3,512,256]{2,3,0,1:T(8,128)} %all-reduce.3.cloned.1.call-done), kind=kOutput, calls=%fused_computation.31 | convolution fusion | flops 4833411072 | bytes 9502768 | tf_op jit(solution)/shard_map/hmrf,hmrg->hmfg/dot_general | solution.py:20
  239.9 6.4 %fusion.36 = f32[4,3,256,256]{3,2,1,0:T(8,128)S(1)} fusion(f32[4,3,256,256]{3,2,1,0:T(8,128)} %get-tuple-element.18, f32[4,3]{1,0:T(4,128)S(1)} %get-tuple-element.15), kind=kOutput, calls=%fused_computation.46 | convolution fusion | flops 2416705536 | bytes 6291504 | tf_op jit(solution)/shard_map/hmfg,hmgk->hmfk/dot_general | solution.py:32
  246.4 10.8 %fusion.2 = f32[4,3,512,256]{3,2,1,0:T(8,128)S(1)} fusion(f32[4,3,256,256]{3,2,1,0:T(8,128)S(1)} %fusion.36, f32[256,256]{1,0:T(8,128)S(1)} %broadcast_select_fusion, f32[4,3,256,256]{3,2,1,0:T(8,128)S(1)} %copy-done.1, f32[4,3]{1,0:T(4,128)S(1)} %get-tuple-element.15, f32[4,3,512,256]{2,3,0,1:T(8,128)S(1)} %bitcast.117, f32[4,3]{0,1:T(4,128)S(1)} %copy.76), kind=kOutput, calls=%fused_computation.4 | convolution fusion | flops 4837343232 | bytes 19136608 | tf_op jit(solution)/shard_map/hmrf,hmfg->hmrg/dot_general | solution.py:34
  257.2 10.6 %fusion.101 = f32[4,3,256,256]{3,2,1,0:T(8,128)S(1)} fusion(f32[4,3,512,256]{3,2,1,0:T(8,128)S(1)} %fusion.2), kind=kOutput, calls=%fused_computation.145 | convolution fusion | flops 4831838208 | bytes 9437184 | tf_op jit(solution)/shard_map/hmrf,hmrg->hmfg/dot_general | solution.py:20
  267.9 3.9 multiply_add_fusion.1
  271.8 8.1 %fusion.100 = (bf16[4,3,512,256]{3,2,0,1:T(8,128)(2,1)S(1)}, f32[4,3,512,256]{3,2,0,1:T(8,128)}) fusion(f32[4,3,512,256]{3,2,0,1:T(8,128)S(1)} %bitcast.115, f32[4,3,256,256]{3,2,1,0:T(8,128)S(1)} %multiply_add_fusion.1, f32[4,3,512,256]{3,2,1,0:T(8,128)S(1)} %fusion.2), kind=kOutput, calls=%fused_computation.144 | convolution fusion | flops 4836556800 | bytes 25165824 | tf_op jit(solution)/shard_map/hmrf,hmfg->hmrg/dot_general | solution.py:34
  282.6 3.3 pad_maximum_fusion.1
  286.0 1.9 fusion.96
  287.9 1.9 all_to_all.95
  289.7 1.7 copy.80
  291.5 4.1 all-to-all-start.3
  295.6 1.9 all_to_all.105
  297.4 1.7 copy.101
  299.1 1.7 all-to-all-done.3
  300.9 4.1 all-to-all-start.7
  305.0 1.9 reshape.93
  306.8 3.4 all-to-all-done.7
  310.2 1.8 reshape.95
  312.1 2.0 convolution_bitcast_fusion.12
  314.0 2.4 fusion.38
  316.4 1.2 copy.83
  318.4 107.0 %all-reduce.5.cloned.1.call-done = f32[4,3,512,256]{2,3,0,1:T(8,128)} async-done(((f32[4,3,512,256]{2,3,0,1:T(8,128)}), f32[4,3,512,256]{2,3,0,1:T(8,128)}) %all-reduce.5.cloned.1.call-update) | async-done | bytes 6291472 | tf_op jit(solution)/shard_map/psum | solution.py:81
  425.5 18.8 %select_reduce_fusion = (f32[4,3]{1,0:T(4,128)S(1)}, f32[4,3,256,256]{3,2,1,0:T(8,128)}) fusion(pred[256,256]{1,0:T(8,128)(4,1)S(1)} %iota_compare_fusion, f32[4,3,512,256]{2,3,0,1:T(8,128)} %all-reduce.5.cloned.1.call-done), kind=kOutput, calls=%fused_computation.24 | convolution fusion | flops 4833411072 | bytes 9502768 | tf_op jit(solution)/shard_map/hmrf,hmrg->hmfg/dot_general | solution.py:20
  444.4 6.7 %fusion.37 = f32[4,3,256,256]{3,2,1,0:T(8,128)S(1)} fusion(f32[4,3,256,256]{3,2,1,0:T(8,128)} %get-tuple-element.22, f32[4,3]{1,0:T(4,128)S(1)} %get-tuple-element.13), kind=kOutput, calls=%fused_computation.47 | convolution fusion | flops 2416705536 | bytes 6291504 | tf_op jit(solution)/shard_map/hmfg,hmgk->hmfk/dot_general | solution.py:32
  451.1 11.4 %fusion = f32[4,3,512,256]{3,2,1,0:T(8,128)S(1)} fusion(f32[4,3,256,256]{3,2,1,0:T(8,128)S(1)} %fusion.37, f32[256,256]{1,0:T(8,128)S(1)} %broadcast_select_fusion, f32[4,3,256,256]{3,2,1,0:T(8,128)S(1)} %copy-done, f32[4,3]{1,0:T(4,128)S(1)} %get-tuple-element.13, f32[4,3,512,256]{2,3,0,1:T(8,128)S(1)} %bitcast.119, f32[4,3]{0,1:T(4,128)S(1)} %copy.97), kind=kOutput, calls=%fused_computation.2 | convolution fusion | flops 4837343232 | bytes 19136608 | tf_op jit(solution)/shard_map/hmrf,hmfg->hmrg/dot_general | solution.py:34
  462.6 10.8 %fusion.102 = f32[4,3,256,256]{3,2,1,0:T(8,128)S(1)} fusion(f32[4,3,512,256]{3,2,1,0:T(8,128)S(1)} %fusion), kind=kOutput, calls=%fused_computation.146 | convolution fusion | flops 4831838208 | bytes 9437184 | tf_op jit(solution)/shard_map/hmrf,hmrg->hmfg/dot_general | solution.py:20
  473.4 4.1 multiply_add_fusion
  477.6 6.5 %subtract_convert_fusion = bf16[4,3,512,256]{3,2,0,1:T(8,128)(2,1)S(1)} fusion(f32[4,3,512,256]{3,2,0,1:T(8,128)S(1)} %bitcast.113, f32[4,3,256,256]{3,2,1,0:T(8,128)S(1)} %multiply_add_fusion, f32[4,3,512,256]{3,2,1,0:T(8,128)S(1)} %fusion), kind=kOutput, calls=%fused_computation.14 | convolution fusion | flops 4836556800 | bytes 18874368 | tf_op jit(solution)/shard_map/hmrf,hmfg->hmrg/dot_general | solution.py:34
  485.2 2.4 fusion.39
  487.5 1.2 copy.104
  (84 shorter events, 16.8 us)
Async XLA Ops:
  6.5 14.7 %copy-start.5 = (bf16[2,32,4096]{2,1,0:T(8,128)(2,1)S(1)}, bf16[2,32,4096]{2,1,0:T(8,128)(2,1)}, u32[]{:S(2)}) copy-start(bf16[2,32,4096]{2,1,0:T(8,128)(2,1)} %param.7) | copy-start | bytes 1572868
  6.5 67.2 %all-gather.2.cloned.1.call-start = ((), (), s32[]{:S(2)}) async-start(), calls=%async_computation.8 | async-start | bytes 6684672 | tf_op jit(solution)/shard_map/all_gather | solution.py:41
  9.7 8.0 %all-to-all-start = ((bf16[32,2,4]{0,2,1:T(4,128)(2,1)}), bf16[32,2,4]{0,2,1:T(4,128)(2,1)S(1)}, u32[]{:S(2)}, u32[]{:S(2)}) async-start(bf16[32,2,4]{0,2,1:T(4,128)(2,1)} %bitcast), calls=%async_computation | async-start | bytes 4096 | tf_op jit(solution)/shard_map/all_to_all | solution.py:50
  17.7 8.6 %all-to-all-start.2 = ((bf16[32,2,2048]{2,0,1:T(8,128)(2,1)}), bf16[32,2,2048]{2,0,1:T(8,128)(2,1)S(1)}, u32[]{:S(2)}, u32[]{:S(2)}) async-start(bf16[32,2,2048]{2,0,1:T(8,128)(2,1)} %copy.67), calls=%async_computation.2 | async-start | bytes 524288 | tf_op jit(solution)/shard_map/all_to_all | solution.py:48
  26.4 8.6 %all-to-all-start.1 = ((bf16[32,2,2048]{2,0,1:T(8,128)(2,1)}), bf16[32,2,2048]{2,0,1:T(8,128)(2,1)S(1)}, u32[]{:S(2)}, u32[]{:S(2)}) async-start(bf16[32,2,2048]{2,0,1:T(8,128)(2,1)} %copy.65), calls=%async_computation.1 | async-start | bytes 524288 | tf_op jit(solution)/shard_map/all_to_all | solution.py:49
  29.8 191.0 %all-reduce.3.cloned.1.call-start = ((), (), s32[]{:S(2)}) async-start(), calls=%async_computation.9 | async-start | bytes 12582912 | tf_op jit(solution)/shard_map/psum | solution.py:81
  82.6 6.8 %all-to-all-start.4 = ((bf16[32,2,4]{0,2,1:T(4,128)(2,1)}), bf16[32,2,4]{0,2,1:T(4,128)(2,1)S(1)}, u32[]{:S(2)}, u32[]{:S(2)}) async-start(bf16[32,2,4]{0,2,1:T(4,128)(2,1)} %bitcast.23), calls=%async_computation.4 | async-start | bytes 4096 | tf_op jit(solution)/shard_map/all_to_all | solution.py:50
  89.5 8.6 %all-to-all-start.5 = ((bf16[32,2,2048]{2,0,1:T(8,128)(2,1)}), bf16[32,2,2048]{2,0,1:T(8,128)(2,1)S(1)}, u32[]{:S(2)}, u32[]{:S(2)}) async-start(bf16[32,2,2048]{2,0,1:T(8,128)(2,1)} %copy.86), calls=%async_computation.5 | async-start | bytes 524288 | tf_op jit(solution)/shard_map/all_to_all | solution.py:49
  98.1 8.6 %all-to-all-start.6 = ((bf16[32,2,2048]{2,0,1:T(8,128)(2,1)}), bf16[32,2,2048]{2,0,1:T(8,128)(2,1)S(1)}, u32[]{:S(2)}, u32[]{:S(2)}) async-start(bf16[32,2,2048]{2,0,1:T(8,128)(2,1)} %copy.88), calls=%async_computation.6 | async-start | bytes 524288 | tf_op jit(solution)/shard_map/all_to_all | solution.py:48
  101.5 324.0 %all-reduce.5.cloned.1.call-start = ((), (), s32[]{:S(2)}) async-start(), calls=%async_computation.10 | async-start | bytes 12582912 | tf_op jit(solution)/shard_map/psum | solution.py:81
  220.8 25.5 %slice-start.4 = ((s8[6291456]{0:T(1024)(128)(4,1)}), s8[2097152]{0:T(1024)(128)(4,1)S(1)}, s32[]{:S(2)}) async-start(s8[6291456]{0:T(1024)(128)(4,1)} %bitcast.116), calls=%async_computation.15 | async-start | bytes 4194304
  239.9 6.4 %slice-start.5 = ((s8[6291456]{0:T(1024)(128)(4,1)}), s8[4194304]{0:T(1024)(128)(4,1)S(1)}, s32[]{:S(2)}) async-start(s8[6291456]{0:T(1024)(128)(4,1)} %bitcast.116), calls=%async_computation.16 | async-start | bytes 8388608
  239.9 6.4 %copy-start.1 = (f32[4,3,256,256]{3,2,1,0:T(8,128)S(1)}, f32[4,3,256,256]{3,2,1,0:T(8,128)}, u32[]{:S(2)}) copy-start(f32[4,3,256,256]{3,2,1,0:T(8,128)} %get-tuple-element.18) | copy-start | bytes 9437188
  239.9 31.8 %slice-start.2 = ((s8[6291456]{0:T(1024)(128)(4,1)}), s8[4194304]{0:T(1024)(128)(4,1)S(1)}, s32[]{:S(2)}) async-start(s8[6291456]{0:T(1024)(128)(4,1)} %bitcast.114), calls=%async_computation.13 | async-start | bytes 8388608
  246.4 25.4 %slice-start.3 = ((s8[6291456]{0:T(1024)(128)(4,1)}), s8[2097152]{0:T(1024)(128)(4,1)S(1)}, s32[]{:S(2)}) async-start(s8[6291456]{0:T(1024)(128)(4,1)} %bitcast.114), calls=%async_computation.14 | async-start | bytes 4194304
  271.8 8.1 %copy-start.2 = (bf16[64,4,512]{2,1,0:T(4,128)(2,1)S(1)}, bf16[64,4,512]{2,1,0:T(4,128)(2,1)}, u32[]{:S(2)}) copy-start(bf16[64,4,512]{2,1,0:T(4,128)(2,1)} %reshape.94) | copy-start | bytes 786436
  279.9 0.9 copy-start.4
  291.5 9.4 %all-to-all-start.3 = ((bf16[32,2,2048]{2,0,1:T(8,128)(2,1)}), bf16[32,2,2048]{2,0,1:T(8,128)(2,1)}, u32[]{:S(2)}, u32[]{:S(2)}) async-start(bf16[32,2,2048]{2,0,1:T(8,128)(2,1)} %copy.80), calls=%async_computation.3 | async-start | bytes 524288 | tf_op jit(solution)/shard_map/all_to_all | solution.py:47
  300.9 9.4 %all-to-all-start.7 = ((bf16[32,2,2048]{2,0,1:T(8,128)(2,1)}), bf16[32,2,2048]{2,0,1:T(8,128)(2,1)}, u32[]{:S(2)}, u32[]{:S(2)}) async-start(bf16[32,2,2048]{2,0,1:T(8,128)(2,1)} %copy.101), calls=%async_computation.7 | async-start | bytes 524288 | tf_op jit(solution)/shard_map/all_to_all | solution.py:47
  425.5 25.6 %slice-start.6 = ((s8[6291456]{0:T(1024)(128)(4,1)}), s8[2097152]{0:T(1024)(128)(4,1)S(1)}, s32[]{:S(2)}) async-start(s8[6291456]{0:T(1024)(128)(4,1)} %bitcast.118), calls=%async_computation.17 | async-start | bytes 4194304
  444.4 6.7 %slice-start.7 = ((s8[6291456]{0:T(1024)(128)(4,1)}), s8[4194304]{0:T(1024)(128)(4,1)S(1)}, s32[]{:S(2)}) async-start(s8[6291456]{0:T(1024)(128)(4,1)} %bitcast.118), calls=%async_computation.18 | async-start | bytes 8388608
  444.4 6.7 %copy-start = (f32[4,3,256,256]{3,2,1,0:T(8,128)S(1)}, f32[4,3,256,256]{3,2,1,0:T(8,128)}, u32[]{:S(2)}) copy-start(f32[4,3,256,256]{3,2,1,0:T(8,128)} %get-tuple-element.22) | copy-start | bytes 9437188
  444.4 33.2 %slice-start = ((s8[6291456]{0:T(1024)(128)(4,1)}), s8[4194304]{0:T(1024)(128)(4,1)S(1)}, s32[]{:S(2)}) async-start(s8[6291456]{0:T(1024)(128)(4,1)} %bitcast.112), calls=%async_computation.11 | async-start | bytes 8388608
  451.1 26.4 %slice-start.1 = ((s8[6291456]{0:T(1024)(128)(4,1)}), s8[2097152]{0:T(1024)(128)(4,1)S(1)}, s32[]{:S(2)}) async-start(s8[6291456]{0:T(1024)(128)(4,1)} %bitcast.112), calls=%async_computation.12 | async-start | bytes 4194304
  477.6 6.6 %copy-start.6 = (bf16[64,4,512]{2,1,0:T(4,128)(2,1)S(1)}, bf16[64,4,512]{2,1,0:T(4,128)(2,1)}, u32[]{:S(2)}) copy-start(bf16[64,4,512]{2,1,0:T(4,128)(2,1)} %reshape.95) | copy-start | bytes 786436
  484.1 4.7 copy-start.3
Sparse Core Ops, SparseCore 0:
  9.5 64.1 all-gather.1
  82.7 137.9 all-reduce.2
  286.1 139.3 all-reduce.4
where the time goes:
time: 502 us; the launch traced here: 497 us
  waiting for transfers between devices  285 us (57%)
  matrix products  130 us (26%)
  starting transfers between devices  29.8 us (6%)
  local copies, waits for them, and re-layouts  26.7 us (5%)
  between operations  14.1 us (3%)
  other arithmetic  11.8 us (2%)
    psum x2, waiting for transfers between devices, local(): total_grad = lax.psum(gradients, 'seq')  219 us
    dot_general x4, matrix products, local_gram(): jnp.einsum('hmrf,hmrg->hmfg', weight_matrices, weight_matrices, precision...  59.2 us
    all_gather x1, waiting for transfers between devices, local(): weights = lax.all_gather(fast_init, 'seq', axis=2, tiled=True)  38.2 us
    dot_general x4, matrix products, newton_schulz(): jnp.einsum('hmrf,hmfg->hmrg', current_weights, polynomial_update, precisi...  36.9 us
    dot_general x4, matrix products, newton_schulz(): jnp.einsum('hmfg,hmgk->hmfk', gram_matrix, gram_matrix, precision=FULL_PR...  21.1 us
  transfers between devices with their start and end apart: 11, of which 11 were waited for; matrix products, arithmetic and copies ran while one was open for 5% of the time, Pallas kernels for 0%

commit v1 on v0

--- a/solution.py
+++ b/solution.py
@@ -45,7 +45,15 @@
     for group_index in range(queries.shape[0]):
         query_flat, key_flat, value_flat, rate_rows = (
             lax.all_to_all(queries[group_index], "head", split_axis=1, concat_axis=0, tiled=True),
-            lax.all_to_all(keys[group_index], "head", split_axis=1, concat_axis=0, tiled=True),
+            jnp.concatenate(
+                lax.all_to_all(
+                    jnp.stack(jnp.split(keys[group_index], lax.axis_size("head"), axis=1)),
+                    "head",
+                    0,
+                    0,
+                ),
+                axis=0,
+            ),
             lax.all_to_all(values[group_index], "head", split_axis=1, concat_axis=0, tiled=True),
             lax.all_to_all(rates[group_index], "head", split_axis=1, concat_axis=0, tiled=True),
         )

time: 502 us -> 492 us (0.980)
  matrix products: 130 us -> 116 us
    dot_general x4, matrix products: 36.9 us -> 28.9 us  [newton_schulz(): jnp.einsum('hmrf,hmfg->hmrg', current_weights, polynomial_update, precisi...]
    dot_general x4, matrix products: 59.2 us -> 53.3 us  [local_gram(): jnp.einsum('hmrf,hmrg->hmfg', weight_matrices, weight_matrices, precision...]
where the time goes in v1:
time: 492 us; the launch traced here: 483 us
  waiting for transfers between devices  285 us (58%)
  matrix products  116 us (24%)
  starting transfers between devices  29.5 us (6%)
  local copies, waits for them, and re-layouts  24.9 us (5%)
  between operations  13.9 us (3%)
  other arithmetic  13.5 us (3%)
    psum x2, waiting for transfers between devices, local(): total_grad = lax.psum(gradients, 'seq')  220 us
    dot_general x4, matrix products, local_gram(): jnp.einsum('hmrf,hmrg->hmfg', weight_matrices, weight_matrices, precision...  53.3 us
    all_gather x1, waiting for transfers between devices, local(): weights = lax.all_gather(fast_init, 'seq', axis=2, tiled=True)  38.4 us
    dot_general x4, matrix products, newton_schulz(): jnp.einsum('hmrf,hmfg->hmrg', current_weights, polynomial_update, precisi...  28.9 us
    dot_general x4, matrix products, newton_schulz(): jnp.einsum('hmfg,hmgk->hmfk', gram_matrix, gram_matrix, precision=FULL_PR...  21.5 us
    all_to_all x2, waiting for transfers between devices, local(): lax.all_to_all(values[group_index], 'head', split_axis=1, concat_axis=0,...  10.1 us
  transfers between devices with their start and end apart: 11, of which 11 were waited for; matrix products, arithmetic and copies ran while one was open for 5% of the time, Pallas kernels for 0%

profile of v1, /device:TPU:0, one launch (start us, length us, event | category | flops | bytes accessed | tf_op | source)
XLA Modules:
  0.0 483.2 jit_solution(17130723074519323378)
XLA Ops:
  6.5 1.8 copy.56
  8.4 1.3 fusion.98
  9.7 4.3 all-to-all-start.1
  13.9 1.1 slice_bitcast_fusion.23
  17.7 3.5 all-to-all-start.2
  21.3 5.1 %all-to-all-done.2 = bf16[32,2,2048]{2,0,1:T(8,128)(2,1)S(1)} async-done(((bf16[32,2,2048]{2,0,1:T(8,128)(2,1)}), bf16[32,2,2048]{2,0,1:T(8,128)(2,1)S(1)}, u32[]{:S(2)}, u32[]{:S(2)}) %all-to-all-start.2) | async-done | bytes 262176 | tf_op jit(solution)/shard_map/all_to_all | solution.py:57
  26.3 3.4 all-to-all-start
  30.3 4.7 all-to-all-done
  35.3 38.4 %all-gather.2.cloned.1.call-done = f32[4,3,512,256]{3,2,0,1:T(8,128)} async-done(((f32[4,3,32,256]{3,2,0,1:T(8,128)}), f32[4,3,512,256]{3,2,0,1:T(8,128)}) %all-gather.2.cloned.1.call-update) | async-done | bytes 6291472 | tf_op jit(solution)/shard_map/all_gather | solution.py:41
  73.7 3.1 convert_element_type.105
  79.3 3.4 pad_maximum_fusion
  82.7 3.2 all-to-all-start.5
  87.7 1.8 all-to-all-done.5
  89.5 3.4 all-to-all-start.6
  93.1 5.1 %all-to-all-done.6 = bf16[32,2,2048]{2,0,1:T(8,128)(2,1)S(1)} async-done(((bf16[32,2,2048]{2,0,1:T(8,128)(2,1)}), bf16[32,2,2048]{2,0,1:T(8,128)(2,1)S(1)}, u32[]{:S(2)}, u32[]{:S(2)}) %all-to-all-start.6) | async-done | bytes 262176 | tf_op jit(solution)/shard_map/all_to_all | solution.py:57
  98.1 3.4 all-to-all-start.4
  102.0 4.7 all-to-all-done.4
  108.5 112.3 %all-reduce.3.cloned.1.call-done = f32[4,3,512,256]{3,2,0,1:T(8,128)} async-done(((f32[4,3,512,256]{3,2,0,1:T(8,128)}), f32[4,3,512,256]{3,2,0,1:T(8,128)}) %all-reduce.3.cloned.1.call-update) | async-done | bytes 6291472 | tf_op jit(solution)/shard_map/psum | solution.py:89
  220.8 15.8 %select_reduce_fusion.1 = (f32[4,3]{1,0:T(4,128)S(1)}, f32[4,3,256,256]{3,2,1,0:T(8,128)}) fusion(pred[256,256]{1,0:T(8,128)(4,1)S(1)} %iota_compare_fusion, f32[4,3,512,256]{3,2,0,1:T(8,128)} %all-reduce.3.cloned.1.call-done), kind=kOutput, calls=%fused_computation.31 | convolution fusion | flops 4833411072 | bytes 9502768 | tf_op jit(solution)/shard_map/hmrf,hmrg->hmfg/dot_general | solution.py:20
  236.8 6.4 %fusion.36 = f32[4,3,256,256]{3,2,1,0:T(8,128)S(1)} fusion(f32[4,3,256,256]{3,2,1,0:T(8,128)} %get-tuple-element.22, f32[4,3]{1,0:T(4,128)S(1)} %get-tuple-element.19), kind=kOutput, calls=%fused_computation.46 | convolution fusion | flops 2416705536 | bytes 6291504 | tf_op jit(solution)/shard_map/hmfg,hmgk->hmfk/dot_general | solution.py:32
  243.2 6.7 %fusion.10 = f32[4,3,512,256]{3,2,1,0:T(8,128)S(1)} fusion(f32[4,3,256,256]{3,2,1,0:T(8,128)S(1)} %fusion.36, f32[256,256]{1,0:T(8,128)S(1)} %broadcast_select_fusion, f32[4,3,256,256]{3,2,1,0:T(8,128)S(1)} %copy-done.1, f32[4,3]{1,0:T(4,128)S(1)} %get-tuple-element.19, f32[4,3,512,256]{3,2,0,1:T(8,128)S(1)} %bitcast.119, f32[4,3]{0,1:T(4,128)S(1)} %copy.68), kind=kOutput, calls=%fused_computation.12 | convolution fusion | flops 4837343232 | bytes 19136608 | tf_op jit(solution)/shard_map/hmrf,hmfg->hmrg/dot_general | solution.py:34
  249.9 10.6 %fusion.100 = f32[4,3,256,256]{3,2,1,0:T(8,128)S(1)} fusion(f32[4,3,512,256]{3,2,1,0:T(8,128)S(1)} %fusion.10), kind=kOutput, calls=%fused_computation.152 | convolution fusion | flops 4831838208 | bytes 9437184 | tf_op jit(solution)/shard_map/hmrf,hmrg->hmfg/dot_general | solution.py:20
  260.6 4.0 multiply_add_fusion.1
  264.7 8.1 %fusion.99 = (bf16[4,3,512,256]{3,2,0,1:T(8,128)(2,1)S(1)}, f32[4,3,512,256]{3,2,0,1:T(8,128)}) fusion(f32[4,3,512,256]{3,2,0,1:T(8,128)S(1)} %bitcast.117, f32[4,3,256,256]{3,2,1,0:T(8,128)S(1)} %multiply_add_fusion.1, f32[4,3,512,256]{3,2,1,0:T(8,128)S(1)} %fusion.10), kind=kOutput, calls=%fused_computation.151 | convolution fusion | flops 4836556800 | bytes 25165824 | tf_op jit(solution)/shard_map/hmrf,hmfg->hmrg/dot_general | solution.py:34
  275.5 3.4 pad_maximum_fusion.1
  278.9 1.9 fusion.96
  280.8 1.9 all_to_all.75
  282.6 1.7 copy.72
  284.4 4.1 all-to-all-start.3
  288.5 1.9 all_to_all.83
  290.3 1.7 copy.91
  292.0 1.7 all-to-all-done.3
  293.8 4.1 all-to-all-start.7
  297.9 1.9 reshape.76
  299.7 3.4 all-to-all-done.7
  303.1 1.8 reshape.77
  305.0 2.0 convolution_bitcast_fusion.12
  306.9 2.4 fusion.38
  309.3 1.2 copy.75
  311.4 107.2 %all-reduce.5.cloned.1.call-done = f32[4,3,512,256]{3,2,0,1:T(8,128)} async-done(((f32[4,3,512,256]{3,2,0,1:T(8,128)}), f32[4,3,512,256]{3,2,0,1:T(8,128)}) %all-reduce.5.cloned.1.call-update) | async-done | bytes 6291472 | tf_op jit(solution)/shard_map/psum | solution.py:89
  418.6 16.1 %select_reduce_fusion = (f32[4,3]{1,0:T(4,128)S(1)}, f32[4,3,256,256]{3,2,1,0:T(8,128)}) fusion(pred[256,256]{1,0:T(8,128)(4,1)S(1)} %iota_compare_fusion, f32[4,3,512,256]{3,2,0,1:T(8,128)} %all-reduce.5.cloned.1.call-done), kind=kOutput, calls=%fused_computation.24 | convolution fusion | flops 4833411072 | bytes 9502768 | tf_op jit(solution)/shard_map/hmrf,hmrg->hmfg/dot_general | solution.py:20
  434.8 6.7 %fusion.37 = f32[4,3,256,256]{3,2,1,0:T(8,128)S(1)} fusion(f32[4,3,256,256]{3,2,1,0:T(8,128)} %get-tuple-element.26, f32[4,3]{1,0:T(4,128)S(1)} %get-tuple-element.17), kind=kOutput, calls=%fused_computation.47 | convolution fusion | flops 2416705536 | bytes 6291504 | tf_op jit(solution)/shard_map/hmfg,hmgk->hmfk/dot_general | solution.py:32
  441.5 7.6 %fusion.8 = f32[4,3,512,256]{3,2,1,0:T(8,128)S(1)} fusion(f32[4,3,256,256]{3,2,1,0:T(8,128)S(1)} %fusion.37, f32[256,256]{1,0:T(8,128)S(1)} %broadcast_select_fusion, f32[4,3,256,256]{3,2,1,0:T(8,128)S(1)} %copy-done, f32[4,3]{1,0:T(4,128)S(1)} %get-tuple-element.17, f32[4,3,512,256]{3,2,0,1:T(8,128)S(1)} %bitcast.121, f32[4,3]{0,1:T(4,128)S(1)} %copy.87), kind=kOutput, calls=%fused_computation.10 | convolution fusion | flops 4837343232 | bytes 19136608 | tf_op jit(solution)/shard_map/hmrf,hmfg->hmrg/dot_general | solution.py:34
  449.1 10.7 %fusion.101 = f32[4,3,256,256]{3,2,1,0:T(8,128)S(1)} fusion(f32[4,3,512,256]{3,2,1,0:T(8,128)S(1)} %fusion.8), kind=kOutput, calls=%fused_computation.153 | convolution fusion | flops 4831838208 | bytes 9437184 | tf_op jit(solution)/shard_map/hmrf,hmrg->hmfg/dot_general | solution.py:20
  459.9 4.3 multiply_add_fusion
  464.2 6.5 %subtract_convert_fusion = bf16[4,3,512,256]{3,2,0,1:T(8,128)(2,1)S(1)} fusion(f32[4,3,512,256]{3,2,0,1:T(8,128)S(1)} %bitcast.115, f32[4,3,256,256]{3,2,1,0:T(8,128)S(1)} %multiply_add_fusion, f32[4,3,512,256]{3,2,1,0:T(8,128)S(1)} %fusion.8), kind=kOutput, calls=%fused_computation.14 | convolution fusion | flops 4836556800 | bytes 18874368 | tf_op jit(solution)/shard_map/hmrf,hmfg->hmrg/dot_general | solution.py:34
  471.8 2.4 fusion.39
  474.2 1.2 copy.94
  (83 shorter events, 15.9 us)
Async XLA Ops:
  6.5 8.5 %copy-start.5 = (bf16[2,32,4096]{2,1,0:T(8,128)(2,1)S(1)}, bf16[2,32,4096]{2,1,0:T(8,128)(2,1)}, u32[]{:S(2)}) copy-start(bf16[2,32,4096]{2,1,0:T(8,128)(2,1)} %param.7) | copy-start | bytes 1572868
  6.5 67.2 %all-gather.2.cloned.1.call-start = ((), (), s32[]{:S(2)}) async-start(), calls=%async_computation.8 | async-start | bytes 6684672 | tf_op jit(solution)/shard_map/all_gather | solution.py:41
  9.7 8.0 %all-to-all-start.1 = ((bf16[32,2,4]{0,2,1:T(4,128)(2,1)}), bf16[32,2,4]{0,2,1:T(4,128)(2,1)S(1)}, u32[]{:S(2)}, u32[]{:S(2)}) async-start(bf16[32,2,4]{0,2,1:T(4,128)(2,1)} %bitcast.3), calls=%async_computation.1 | async-start | bytes 4096 | tf_op jit(solution)/shard_map/all_to_all | solution.py:58
  17.7 8.6 %all-to-all-start.2 = ((bf16[32,2,2048]{2,0,1:T(8,128)(2,1)}), bf16[32,2,2048]{2,0,1:T(8,128)(2,1)S(1)}, u32[]{:S(2)}, u32[]{:S(2)}) async-start(bf16[32,2,2048]{2,0,1:T(8,128)(2,1)} %copy.59), calls=%async_computation.2 | async-start | bytes 524288 | tf_op jit(solution)/shard_map/all_to_all | solution.py:57
  26.3 8.6 %all-to-all-start = ((bf16[2,32,2048]{2,1,0:T(8,128)(2,1)}), bf16[2,32,2048]{2,1,0:T(8,128)(2,1)S(1)}, u32[]{:S(2)}, u32[]{:S(2)}) async-start(bf16[2,32,2048]{2,1,0:T(8,128)(2,1)} %pad_maximum_fusion.3), calls=%async_computation | async-start | bytes 524288 | tf_op jit(solution)/shard_map/all_to_all | solution.py:49
  29.8 191.0 %all-reduce.3.cloned.1.call-start = ((), (), s32[]{:S(2)}) async-start(), calls=%async_computation.9 | async-start | bytes 12582912 | tf_op jit(solution)/shard_map/psum | solution.py:89
  82.7 6.8 %all-to-all-start.5 = ((bf16[32,2,4]{0,2,1:T(4,128)(2,1)}), bf16[32,2,4]{0,2,1:T(4,128)(2,1)S(1)}, u32[]{:S(2)}, u32[]{:S(2)}) async-start(bf16[32,2,4]{0,2,1:T(4,128)(2,1)} %bitcast.26), calls=%async_computation.5 | async-start | bytes 4096 | tf_op jit(solution)/shard_map/all_to_all | solution.py:58
  89.5 8.6 %all-to-all-start.6 = ((bf16[32,2,2048]{2,0,1:T(8,128)(2,1)}), bf16[32,2,2048]{2,0,1:T(8,128)(2,1)S(1)}, u32[]{:S(2)}, u32[]{:S(2)}) async-start(bf16[32,2,2048]{2,0,1:T(8,128)(2,1)} %copy.78), calls=%async_computation.6 | async-start | bytes 524288 | tf_op jit(solution)/shard_map/all_to_all | solution.py:57
  98.1 8.6 %all-to-all-start.4 = ((bf16[2,32,2048]{2,1,0:T(8,128)(2,1)}), bf16[2,32,2048]{2,1,0:T(8,128)(2,1)S(1)}, u32[]{:S(2)}, u32[]{:S(2)}) async-start(bf16[2,32,2048]{2,1,0:T(8,128)(2,1)} %pad_maximum_fusion.4), calls=%async_computation.4 | async-start | bytes 524288 | tf_op jit(solution)/shard_map/all_to_all | solution.py:49
  101.6 317.0 %all-reduce.5.cloned.1.call-start = ((), (), s32[]{:S(2)}) async-start(), calls=%async_computation.10 | async-start | bytes 12582912 | tf_op jit(solution)/shard_map/psum | solution.py:89
  220.8 22.4 %slice-start.4 = ((s8[6291456]{0:T(1024)(128)(4,1)}), s8[2097152]{0:T(1024)(128)(4,1)S(1)}, s32[]{:S(2)}) async-start(s8[6291456]{0:T(1024)(128)(4,1)} %bitcast.118), calls=%async_computation.15 | async-start | bytes 4194304
  236.8 6.4 %slice-start.5 = ((s8[6291456]{0:T(1024)(128)(4,1)}), s8[4194304]{0:T(1024)(128)(4,1)S(1)}, s32[]{:S(2)}) async-start(s8[6291456]{0:T(1024)(128)(4,1)} %bitcast.118), calls=%async_computation.16 | async-start | bytes 8388608
  236.8 6.4 %copy-start.1 = (f32[4,3,256,256]{3,2,1,0:T(8,128)S(1)}, f32[4,3,256,256]{3,2,1,0:T(8,128)}, u32[]{:S(2)}) copy-start(f32[4,3,256,256]{3,2,1,0:T(8,128)} %get-tuple-element.22) | copy-start | bytes 9437188
  236.8 27.9 %slice-start.2 = ((s8[6291456]{0:T(1024)(128)(4,1)}), s8[4194304]{0:T(1024)(128)(4,1)S(1)}, s32[]{:S(2)}) async-start(s8[6291456]{0:T(1024)(128)(4,1)} %bitcast.116), calls=%async_computation.13 | async-start | bytes 8388608
  243.2 21.4 %slice-start.3 = ((s8[6291456]{0:T(1024)(128)(4,1)}), s8[2097152]{0:T(1024)(128)(4,1)S(1)}, s32[]{:S(2)}) async-start(s8[6291456]{0:T(1024)(128)(4,1)} %bitcast.116), calls=%async_computation.14 | async-start | bytes 4194304
  264.7 8.1 %copy-start.2 = (bf16[64,4,512]{2,1,0:T(4,128)(2,1)S(1)}, bf16[64,4,512]{2,1,0:T(4,128)(2,1)}, u32[]{:S(2)}) copy-start(bf16[64,4,512]{2,1,0:T(4,128)(2,1)} %reshape_reshape.7) | copy-start | bytes 786436
  272.8 0.9 copy-start.4
  284.4 9.4 %all-to-all-start.3 = ((bf16[32,2,2048]{2,0,1:T(8,128)(2,1)}), bf16[32,2,2048]{2,0,1:T(8,128)(2,1)}, u32[]{:S(2)}, u32[]{:S(2)}) async-start(bf16[32,2,2048]{2,0,1:T(8,128)(2,1)} %copy.72), calls=%async_computation.3 | async-start | bytes 524288 | tf_op jit(solution)/shard_map/all_to_all | solution.py:47
  293.8 9.4 %all-to-all-start.7 = ((bf16[32,2,2048]{2,0,1:T(8,128)(2,1)}), bf16[32,2,2048]{2,0,1:T(8,128)(2,1)}, u32[]{:S(2)}, u32[]{:S(2)}) async-start(bf16[32,2,2048]{2,0,1:T(8,128)(2,1)} %copy.91), calls=%async_computation.7 | async-start | bytes 524288 | tf_op jit(solution)/shard_map/all_to_all | solution.py:47
  418.6 22.9 %slice-start.6 = ((s8[6291456]{0:T(1024)(128)(4,1)}), s8[2097152]{0:T(1024)(128)(4,1)S(1)}, s32[]{:S(2)}) async-start(s8[6291456]{0:T(1024)(128)(4,1)} %bitcast.120), calls=%async_computation.17 | async-start | bytes 4194304
  434.8 6.7 %slice-start.7 = ((s8[6291456]{0:T(1024)(128)(4,1)}), s8[4194304]{0:T(1024)(128)(4,1)S(1)}, s32[]{:S(2)}) async-start(s8[6291456]{0:T(1024)(128)(4,1)} %bitcast.120), calls=%async_computation.18 | async-start | bytes 8388608
  434.8 6.7 %copy-start = (f32[4,3,256,256]{3,2,1,0:T(8,128)S(1)}, f32[4,3,256,256]{3,2,1,0:T(8,128)}, u32[]{:S(2)}) copy-start(f32[4,3,256,256]{3,2,1,0:T(8,128)} %get-tuple-element.26) | copy-start | bytes 9437188
  434.8 29.4 %slice-start = ((s8[6291456]{0:T(1024)(128)(4,1)}), s8[4194304]{0:T(1024)(128)(4,1)S(1)}, s32[]{:S(2)}) async-start(s8[6291456]{0:T(1024)(128)(4,1)} %bitcast.114), calls=%async_computation.11 | async-start | bytes 8388608
  441.5 22.7 %slice-start.1 = ((s8[6291456]{0:T(1024)(128)(4,1)}), s8[2097152]{0:T(1024)(128)(4,1)S(1)}, s32[]{:S(2)}) async-start(s8[6291456]{0:T(1024)(128)(4,1)} %bitcast.114), calls=%async_computation.12 | async-start | bytes 4194304
  464.2 6.6 %copy-start.6 = (bf16[64,4,512]{2,1,0:T(4,128)(2,1)S(1)}, bf16[64,4,512]{2,1,0:T(4,128)(2,1)}, u32[]{:S(2)}) copy-start(bf16[64,4,512]{2,1,0:T(4,128)(2,1)} %reshape.77) | copy-start | bytes 786436
  470.8 4.7 copy-start.3
Sparse Core Ops, SparseCore 0:
  9.5 64.1 all-gather.1
  82.8 137.9 all-reduce.2
  279.0 139.5 all-reduce.4
